TPU v7x, 128 devices: a whole 4x4x4 slice. The times are simulated.
128 devices in a mesh: tok: 32 (over y, x, core), kv: 4 (over z).
Axes of the slice: x: 4, y: 4, z: 4, core: 2. Of those that a mesh axis runs over, the one named last changes fastest.
Arguments:
- queries: bfloat16 [8192, 8192], P('tok', 'kv'), may hold values from -12 to 12
- key_states: bfloat16 [8192, 1024], P('tok', 'kv'), may hold values from -12 to 12
- value_states: bfloat16 [8192, 1024], P('tok', 'kv'), may hold values from -6 to 6
- doc_lengths: int32 [16], replicated, may hold values from 1 to 4096, 8192 in all
- block_plan: int32 [32, 32], replicated, may hold values from 0 to 31, each once within a row
Outputs:
- attention_out: bfloat16 [8192, 8192], P(('tok', 'kv'))
- served_lse: float32 [64, 8192], P('kv', 'tok')
Inputs may be any that keep to these rules, and one draw needn't show every extreme that they name: `doc_lengths`: positive lengths that sum to 8192; the largest is exactly 4096. Every row of block_plan is a permutation of 0 to 31.
All inputs are finite; a program needn't handle non-finite values.
Results may differ from a plain program's by a relative error of at most 0.012.
The roundings to bfloat16 on the way count: a program that leaves them out, or rounds other values in their place, can miss the bound.
Values may be sent and summed in bfloat16 or wider, within the bound.
A program may use at most 64 MiB of HBM per device.

v0:
```python
from functools import partial
import math
import jax
import jax.numpy as jnp
from jax import lax
from jax.sharding import PartitionSpec as P

HEAD_DIM = 128
THETA = 500000.0
NEG = -1e30


def doc_layout(doc_lengths, token_index):
    doc_ends = jnp.cumsum(doc_lengths)
    passed = token_index[:, None] >= doc_ends[None, :]
    doc_ids = jnp.sum(passed.astype(jnp.int32), axis=1)
    starts = jnp.sum(jnp.where(passed, doc_lengths[None, :], 0), axis=1)
    return (doc_ids, token_index - starts)


def rotate(inputs, positions, heads):
    half_dim = HEAD_DIM // 2
    inv_freq = jnp.power(
        jnp.float32(THETA), -(jnp.arange(half_dim, dtype=jnp.float32) * 2.0 / HEAD_DIM)
    )
    angles = positions.astype(jnp.float32)[:, None] * inv_freq[None, :]
    cosine = jnp.cos(angles)[:, None, :]
    sine_val = jnp.sin(angles)[:, None, :]
    shaped = inputs.astype(jnp.float32).reshape(inputs.shape[0], heads, HEAD_DIM)
    leading = shaped[..., :half_dim]
    trailing = shaped[..., half_dim:]
    turned = jnp.concatenate(
        [leading * cosine - trailing * sine_val, trailing * cosine + leading * sine_val], axis=-1
    )
    return turned.reshape(inputs.shape[0], heads * HEAD_DIM).astype(jnp.bfloat16)


def attend_block(
    carry_state, query_rows, query_index, query_docs, key_rows, value_rows, key_index, key_docs
):
    row_max, row_sum, weighted = carry_state
    score_scale = 1.0 / math.sqrt(HEAD_DIM)
    scores = (
        jnp.einsum("rgqd,ngd->gqrn", query_rows, key_rows, preferred_element_type=jnp.float32)
        * score_scale
    )
    allowed = (
        (query_docs[:, None] == key_docs[None, :])
        & (key_index[None, :] <= query_index[:, None])
        & (key_index[None, :] >= 0)
    )
    scores = jnp.where(allowed, scores, NEG)
    new_max = jnp.maximum(row_max, jnp.max(scores, axis=-1))
    weights = jnp.where(allowed, jnp.exp(scores - new_max[..., None]), 0.0)
    factor = jnp.exp(row_max - new_max)
    row_sum = row_sum * factor + jnp.sum(weights, axis=-1)
    probs = weights.astype(jnp.bfloat16)
    weighted = weighted * factor[..., None] + jnp.einsum(
        "gqrn,ngd->gqrd", probs, value_rows, preferred_element_type=jnp.float32
    )
    return (new_max, row_sum, weighted)


def fold_keys(
    carry_state, piece, start, query_rows=None, query_index=None, query_docs=None, doc_lengths=None
):
    key_piece, value_piece = piece
    count = key_piece.shape[0]
    stride = math.gcd(count, 512)
    kv_local = key_piece.shape[1] // HEAD_DIM

    def inner(counter, running):
        offset = counter * stride
        key_rows = lax.dynamic_slice_in_dim(key_piece, offset, stride, 0).reshape(
            stride, kv_local, HEAD_DIM
        )
        value_rows = lax.dynamic_slice_in_dim(value_piece, offset, stride, 0).reshape(
            stride, kv_local, HEAD_DIM
        )
        key_index = offset + jnp.arange(stride, dtype=jnp.int32)
        key_docs, unused_pos = doc_layout(doc_lengths, key_index)
        return attend_block(
            running, query_rows, query_index, query_docs, key_rows, value_rows, key_index, key_docs
        )

    return lax.fori_loop(0, count // stride, inner, carry_state)


def finish(carry_state, rows, q_local):
    row_max, row_sum, weighted = carry_state
    mixed = weighted / row_sum[..., None]
    result = (
        jnp.transpose(mixed, (2, 0, 1, 3)).reshape(rows, q_local * HEAD_DIM).astype(jnp.bfloat16)
    )
    log_norm = (row_max + jnp.log(row_sum)).reshape(q_local, rows)
    return (result, log_norm)


def body(queries, key_states, value_states, doc_lengths, block_plan):
    shards = lax.axis_size("tok")
    shard_index = lax.axis_index("tok")
    tok_dev = queries.shape[0]
    block_rows = tok_dev // shards
    kv_local = key_states.shape[1] // HEAD_DIM
    q_local = queries.shape[1] // HEAD_DIM
    per_group = q_local // kv_local
    token_index = shard_index * tok_dev + jnp.arange(tok_dev, dtype=jnp.int32)
    doc_ids, positions = doc_layout(doc_lengths, token_index)
    q_rot = rotate(queries, positions, q_local)
    k_rot = rotate(key_states, positions, kv_local)
    my_blocks = lax.dynamic_index_in_dim(block_plan, shard_index, 0, keepdims=False)
    initial = (
        jnp.full((kv_local, per_group, tok_dev), NEG, jnp.float32),
        jnp.zeros((kv_local, per_group, tok_dev), jnp.float32),
        jnp.zeros((kv_local, per_group, tok_dev, HEAD_DIM), jnp.float32),
    )
    plan_column = lax.dynamic_index_in_dim(block_plan, shard_index, 1, keepdims=False)
    outgoing = jnp.take(q_rot.reshape(shards, block_rows, q_local * HEAD_DIM), my_blocks, axis=0)
    incoming = lax.all_to_all(outgoing, "tok", split_axis=0, concat_axis=0, tiled=True)
    served_index = (
        jnp.arange(shards, dtype=jnp.int32)[:, None] * tok_dev
        + plan_column[:, None] * block_rows
        + jnp.arange(block_rows, dtype=jnp.int32)[None, :]
    ).reshape(tok_dev)
    served_docs, unused_pos = doc_layout(doc_lengths, served_index)
    served_rows = incoming.reshape(tok_dev, kv_local, per_group, HEAD_DIM)
    folder = partial(
        fold_keys,
        query_rows=served_rows,
        query_index=served_index,
        query_docs=served_docs,
        doc_lengths=doc_lengths,
    )
    final_state = folder(
        initial,
        (
            lax.all_gather(k_rot, "tok", axis=0, tiled=True),
            lax.all_gather(value_states, "tok", axis=0, tiled=True),
        ),
        jnp.int32(0),
    )
    result, served_lse = finish(final_state, tok_dev, q_local)
    returned = lax.all_to_all(
        result.reshape(shards, block_rows, q_local * HEAD_DIM),
        "tok",
        split_axis=0,
        concat_axis=0,
        tiled=True,
    )
    ordered = (
        jnp.zeros_like(returned).at[my_blocks].set(returned).reshape(tok_dev, q_local * HEAD_DIM)
    )
    attention_out = lax.all_to_all(ordered, "kv", split_axis=0, concat_axis=1, tiled=True)
    return (attention_out, served_lse)


def solution(mesh):
    return jax.shard_map(
        body,
        mesh=mesh,
        in_specs=(P("tok", "kv"), P("tok", "kv"), P("tok", "kv"), P(), P()),
        out_specs=(P(("tok", "kv"), None), P("kv", "tok")),
        check_vma=False,
    )
```

profile of v0, /device:TPU:0, one launch (start us, length us, event | category | flops | bytes accessed | tf_op | source)
XLA Modules:
  0.0 487.8 jit_solution(9570828459599723917)
XLA Ops:
  7.2 1.6 add_reduce_fusion
  9.7 1.4 broadcast_in_dim.111
  11.0 1.3 select_reduce_fusion
  14.4 1.7 copy.36
  22.5 7.6 %all-to-all-start = ((bf16[32,8,2048]{2,1,0:T(8,128)(2,1)}), bf16[32,8,2048]{2,1,0:T(8,128)(2,1)S(1)}, u32[]{:S(2)}, u32[]{:S(2)}) async-start(bf16[32,8,2048]{2,1,0:T(8,128)(2,1)} %broadcast_select_fusion), calls=%async_computation | async-start | bytes 2097152 | tf_op jit(solution)/shard_map/all_to_all | solution.py:119
  30.1 18.3 %all-to-all-done = bf16[32,8,2048]{2,1,0:T(8,128)(2,1)S(1)} async-done(((bf16[32,8,2048]{2,1,0:T(8,128)(2,1)}), bf16[32,8,2048]{2,1,0:T(8,128)(2,1)S(1)}, u32[]{:S(2)}, u32[]{:S(2)}) %all-to-all-start) | async-done | bytes 1048608 | tf_op jit(solution)/shard_map/all_to_all | solution.py:119
  48.9 24.8 %all-gather.3.cloned.1.call-done = bf16[8192,256]{0,1:T(8,128)(2,1)} async-done(((bf16[256,256]{0,1:T(8,128)(2,1)}), bf16[8192,256]{0,1:T(8,128)(2,1)}) %all-gather.3.cloned.1.call-update) | async-done | bytes 4194320 | tf_op jit(solution)/shard_map/all_gather | solution.py:137
  73.7 50.9 %all-gather.5.cloned.1.call-done = bf16[8192,256]{0,1:T(8,128)(2,1)} async-done(((bf16[256,256]{0,1:T(8,128)(2,1)}), bf16[8192,256]{0,1:T(8,128)(2,1)}) %all-gather.5.cloned.1.call-update) | async-done | bytes 4194320 | tf_op jit(solution)/shard_map/all_gather | solution.py:138
  124.6 304.6 %while.20 = (s32[]{:T(128)}, f32[2,8,256]{2,1,0:T(8,128)S(1)}, f32[2,8,256]{2,1,0:T(8,128)}, f32[2,8,256,128]{3,2,1,0:T(8,128)S(1)}, s32[256]{0:T(256)}, /*index...) while((s32[]{:T(128)}, f32[2,8,256]{2,1,0:T(8,128)S(1)}, ...), condition=%wide.region_7.8_spmd.clone, body=%wide.region_3.7_spmd.clone.sunk | while | flops 1103148288 | bytes 66470364 | solution.py:86
  128.2 5.3 %fusion.32 = (f32[2,8,256]{2,1,0:T(8,128)}, f32[2,512,256,8]{2,1,3,0:T(8,128)}) fusion(pred[256,512]{0,1:T(8,128)(4,1)S(1)} %and_and_fusion.2, bf16[512,2,128,1]{0,2,3,1:T(8,128)(2,1)S(1)} %bitcast.72, bf16[256,2,8,128]{3,0,2,1:T(8,128)(2,1)S(1)} %get-tuple-element.448), kind=kOutput, calls=%fused_computation.5.clone.1 | convolution fusion | flops 543158272 | bytes 9846784 | tf_op jit(solution)/shard_map/while/body/eval_jaxpr/rgqd,ngd->gqrn/dot_general | solution.py:44
  134.3 4.6 fusion.33
  138.9 1.2 copy-done
  140.1 3.5 fusion.35
  147.3 5.3 %fusion.32 = (f32[2,8,256]{2,1,0:T(8,128)}, f32[2,512,256,8]{2,1,3,0:T(8,128)}) fusion(pred[256,512]{0,1:T(8,128)(4,1)S(1)} %and_and_fusion.2, bf16[512,2,128,1]{0,2,3,1:T(8,128)(2,1)S(1)} %bitcast.72, bf16[256,2,8,128]{3,0,2,1:T(8,128)(2,1)S(1)} %get-tuple-element.448), kind=kOutput, calls=%fused_computation.5.clone.1 | convolution fusion | flops 543158272 | bytes 9846784 | tf_op jit(solution)/shard_map/while/body/eval_jaxpr/rgqd,ngd->gqrn/dot_general | solution.py:44
  153.3 4.6 fusion.33
  158.0 1.2 copy-done
  159.2 3.5 fusion.35
  166.3 5.3 %fusion.32 = (f32[2,8,256]{2,1,0:T(8,128)}, f32[2,512,256,8]{2,1,3,0:T(8,128)}) fusion(pred[256,512]{0,1:T(8,128)(4,1)S(1)} %and_and_fusion.2, bf16[512,2,128,1]{0,2,3,1:T(8,128)(2,1)S(1)} %bitcast.72, bf16[256,2,8,128]{3,0,2,1:T(8,128)(2,1)S(1)} %get-tuple-element.448), kind=kOutput, calls=%fused_computation.5.clone.1 | convolution fusion | flops 543158272 | bytes 9846784 | tf_op jit(solution)/shard_map/while/body/eval_jaxpr/rgqd,ngd->gqrn/dot_general | solution.py:44
  172.4 4.6 fusion.33
  178.2 3.5 fusion.35
  185.3 5.3 %fusion.32 = (f32[2,8,256]{2,1,0:T(8,128)}, f32[2,512,256,8]{2,1,3,0:T(8,128)}) fusion(pred[256,512]{0,1:T(8,128)(4,1)S(1)} %and_and_fusion.2, bf16[512,2,128,1]{0,2,3,1:T(8,128)(2,1)S(1)} %bitcast.72, bf16[256,2,8,128]{3,0,2,1:T(8,128)(2,1)S(1)} %get-tuple-element.448), kind=kOutput, calls=%fused_computation.5.clone.1 | convolution fusion | flops 543158272 | bytes 9846784 | tf_op jit(solution)/shard_map/while/body/eval_jaxpr/rgqd,ngd->gqrn/dot_general | solution.py:44
  191.4 4.6 fusion.33
  197.3 3.5 fusion.35
  204.4 5.3 %fusion.32 = (f32[2,8,256]{2,1,0:T(8,128)}, f32[2,512,256,8]{2,1,3,0:T(8,128)}) fusion(pred[256,512]{0,1:T(8,128)(4,1)S(1)} %and_and_fusion.2, bf16[512,2,128,1]{0,2,3,1:T(8,128)(2,1)S(1)} %bitcast.72, bf16[256,2,8,128]{3,0,2,1:T(8,128)(2,1)S(1)} %get-tuple-element.448), kind=kOutput, calls=%fused_computation.5.clone.1 | convolution fusion | flops 543158272 | bytes 9846784 | tf_op jit(solution)/shard_map/while/body/eval_jaxpr/rgqd,ngd->gqrn/dot_general | solution.py:44
  210.4 4.6 fusion.33
  216.3 3.5 fusion.35
  223.4 5.3 %fusion.32 = (f32[2,8,256]{2,1,0:T(8,128)}, f32[2,512,256,8]{2,1,3,0:T(8,128)}) fusion(pred[256,512]{0,1:T(8,128)(4,1)S(1)} %and_and_fusion.2, bf16[512,2,128,1]{0,2,3,1:T(8,128)(2,1)S(1)} %bitcast.72, bf16[256,2,8,128]{3,0,2,1:T(8,128)(2,1)S(1)} %get-tuple-element.448), kind=kOutput, calls=%fused_computation.5.clone.1 | convolution fusion | flops 543158272 | bytes 9846784 | tf_op jit(solution)/shard_map/while/body/eval_jaxpr/rgqd,ngd->gqrn/dot_general | solution.py:44
  229.5 4.6 fusion.33
  235.3 3.5 fusion.35
  242.5 5.3 %fusion.32 = (f32[2,8,256]{2,1,0:T(8,128)}, f32[2,512,256,8]{2,1,3,0:T(8,128)}) fusion(pred[256,512]{0,1:T(8,128)(4,1)S(1)} %and_and_fusion.2, bf16[512,2,128,1]{0,2,3,1:T(8,128)(2,1)S(1)} %bitcast.72, bf16[256,2,8,128]{3,0,2,1:T(8,128)(2,1)S(1)} %get-tuple-element.448), kind=kOutput, calls=%fused_computation.5.clone.1 | convolution fusion | flops 543158272 | bytes 9846784 | tf_op jit(solution)/shard_map/while/body/eval_jaxpr/rgqd,ngd->gqrn/dot_general | solution.py:44
  248.5 4.6 fusion.33
  254.4 3.5 fusion.35
  261.5 5.3 %fusion.32 = (f32[2,8,256]{2,1,0:T(8,128)}, f32[2,512,256,8]{2,1,3,0:T(8,128)}) fusion(pred[256,512]{0,1:T(8,128)(4,1)S(1)} %and_and_fusion.2, bf16[512,2,128,1]{0,2,3,1:T(8,128)(2,1)S(1)} %bitcast.72, bf16[256,2,8,128]{3,0,2,1:T(8,128)(2,1)S(1)} %get-tuple-element.448), kind=kOutput, calls=%fused_computation.5.clone.1 | convolution fusion | flops 543158272 | bytes 9846784 | tf_op jit(solution)/shard_map/while/body/eval_jaxpr/rgqd,ngd->gqrn/dot_general | solution.py:44
  267.6 4.6 fusion.33
  273.4 3.5 fusion.35
  280.5 5.3 %fusion.32 = (f32[2,8,256]{2,1,0:T(8,128)}, f32[2,512,256,8]{2,1,3,0:T(8,128)}) fusion(pred[256,512]{0,1:T(8,128)(4,1)S(1)} %and_and_fusion.2, bf16[512,2,128,1]{0,2,3,1:T(8,128)(2,1)S(1)} %bitcast.72, bf16[256,2,8,128]{3,0,2,1:T(8,128)(2,1)S(1)} %get-tuple-element.448), kind=kOutput, calls=%fused_computation.5.clone.1 | convolution fusion | flops 543158272 | bytes 9846784 | tf_op jit(solution)/shard_map/while/body/eval_jaxpr/rgqd,ngd->gqrn/dot_general | solution.py:44
  286.6 4.6 fusion.33
  292.5 3.5 fusion.35
  299.6 5.3 %fusion.32 = (f32[2,8,256]{2,1,0:T(8,128)}, f32[2,512,256,8]{2,1,3,0:T(8,128)}) fusion(pred[256,512]{0,1:T(8,128)(4,1)S(1)} %and_and_fusion.2, bf16[512,2,128,1]{0,2,3,1:T(8,128)(2,1)S(1)} %bitcast.72, bf16[256,2,8,128]{3,0,2,1:T(8,128)(2,1)S(1)} %get-tuple-element.448), kind=kOutput, calls=%fused_computation.5.clone.1 | convolution fusion | flops 543158272 | bytes 9846784 | tf_op jit(solution)/shard_map/while/body/eval_jaxpr/rgqd,ngd->gqrn/dot_general | solution.py:44
  305.6 4.6 fusion.33
  311.5 3.5 fusion.35
  318.6 5.3 %fusion.32 = (f32[2,8,256]{2,1,0:T(8,128)}, f32[2,512,256,8]{2,1,3,0:T(8,128)}) fusion(pred[256,512]{0,1:T(8,128)(4,1)S(1)} %and_and_fusion.2, bf16[512,2,128,1]{0,2,3,1:T(8,128)(2,1)S(1)} %bitcast.72, bf16[256,2,8,128]{3,0,2,1:T(8,128)(2,1)S(1)} %get-tuple-element.448), kind=kOutput, calls=%fused_computation.5.clone.1 | convolution fusion | flops 543158272 | bytes 9846784 | tf_op jit(solution)/shard_map/while/body/eval_jaxpr/rgqd,ngd->gqrn/dot_general | solution.py:44
  324.7 4.6 fusion.33
  330.5 3.5 fusion.35
  337.7 5.3 %fusion.32 = (f32[2,8,256]{2,1,0:T(8,128)}, f32[2,512,256,8]{2,1,3,0:T(8,128)}) fusion(pred[256,512]{0,1:T(8,128)(4,1)S(1)} %and_and_fusion.2, bf16[512,2,128,1]{0,2,3,1:T(8,128)(2,1)S(1)} %bitcast.72, bf16[256,2,8,128]{3,0,2,1:T(8,128)(2,1)S(1)} %get-tuple-element.448), kind=kOutput, calls=%fused_computation.5.clone.1 | convolution fusion | flops 543158272 | bytes 9846784 | tf_op jit(solution)/shard_map/while/body/eval_jaxpr/rgqd,ngd->gqrn/dot_general | solution.py:44
  343.7 4.6 fusion.33
  349.6 3.5 fusion.35
  356.7 5.3 %fusion.32 = (f32[2,8,256]{2,1,0:T(8,128)}, f32[2,512,256,8]{2,1,3,0:T(8,128)}) fusion(pred[256,512]{0,1:T(8,128)(4,1)S(1)} %and_and_fusion.2, bf16[512,2,128,1]{0,2,3,1:T(8,128)(2,1)S(1)} %bitcast.72, bf16[256,2,8,128]{3,0,2,1:T(8,128)(2,1)S(1)} %get-tuple-element.448), kind=kOutput, calls=%fused_computation.5.clone.1 | convolution fusion | flops 543158272 | bytes 9846784 | tf_op jit(solution)/shard_map/while/body/eval_jaxpr/rgqd,ngd->gqrn/dot_general | solution.py:44
  362.8 4.6 fusion.33
  368.6 3.5 fusion.35
  375.7 5.3 %fusion.32 = (f32[2,8,256]{2,1,0:T(8,128)}, f32[2,512,256,8]{2,1,3,0:T(8,128)}) fusion(pred[256,512]{0,1:T(8,128)(4,1)S(1)} %and_and_fusion.2, bf16[512,2,128,1]{0,2,3,1:T(8,128)(2,1)S(1)} %bitcast.72, bf16[256,2,8,128]{3,0,2,1:T(8,128)(2,1)S(1)} %get-tuple-element.448), kind=kOutput, calls=%fused_computation.5.clone.1 | convolution fusion | flops 543158272 | bytes 9846784 | tf_op jit(solution)/shard_map/while/body/eval_jaxpr/rgqd,ngd->gqrn/dot_general | solution.py:44
  381.8 4.6 fusion.33
  387.7 3.5 fusion.35
  394.8 5.3 %fusion.32 = (f32[2,8,256]{2,1,0:T(8,128)}, f32[2,512,256,8]{2,1,3,0:T(8,128)}) fusion(pred[256,512]{0,1:T(8,128)(4,1)S(1)} %and_and_fusion.2, bf16[512,2,128,1]{0,2,3,1:T(8,128)(2,1)S(1)} %bitcast.72, bf16[256,2,8,128]{3,0,2,1:T(8,128)(2,1)S(1)} %get-tuple-element.448), kind=kOutput, calls=%fused_computation.5.clone.1 | convolution fusion | flops 543158272 | bytes 9846784 | tf_op jit(solution)/shard_map/while/body/eval_jaxpr/rgqd,ngd->gqrn/dot_general | solution.py:44
  400.8 4.6 fusion.33
  406.7 3.5 fusion.35
  413.8 5.3 %fusion.32 = (f32[2,8,256]{2,1,0:T(8,128)}, f32[2,512,256,8]{2,1,3,0:T(8,128)}) fusion(pred[256,512]{0,1:T(8,128)(4,1)S(1)} %and_and_fusion.2, bf16[512,2,128,1]{0,2,3,1:T(8,128)(2,1)S(1)} %bitcast.72, bf16[256,2,8,128]{3,0,2,1:T(8,128)(2,1)S(1)} %get-tuple-element.448), kind=kOutput, calls=%fused_computation.5.clone.1 | convolution fusion | flops 543158272 | bytes 9846784 | tf_op jit(solution)/shard_map/while/body/eval_jaxpr/rgqd,ngd->gqrn/dot_general | solution.py:44
  419.9 4.6 fusion.33
  425.7 3.5 fusion.35
  429.3 1.4 fusion.15
  431.9 22.5 %all_to_all.29 = bf16[32,8,2048]{2,1,0:T(8,128)(2,1)S(1)} all-to-all(bf16[32,8,2048]{2,1,0:T(8,128)(2,1)S(1)} %convert_element_type.56), channel_id=1, replica_groups=mesh['tok'=32,'kv'=4] {'tok'}, dimensions={0} | all-to-all | bytes 2097152 | tf_op jit(solution)/shard_map/all_to_all | solution.py:143
  455.5 4.6 scatter_fusion
  460.1 4.4 all-to-all-start.2
  465.1 14.8 %all-to-all-done.2 = bf16[4,64,2048]{2,1,0:T(8,128)(2,1)S(1)} async-done(((bf16[4,64,2048]{2,1,0:T(8,128)(2,1)}), bf16[4,64,2048]{2,1,0:T(8,128)(2,1)S(1)}, u32[]{:S(2)}, u32[]{:S(2)}) %all-to-all-start.2) | async-done | bytes 1048608 | tf_op jit(solution)/shard_map/all_to_all | solution.py:153
  (297 shorter events, 99.8 us)
Async XLA Ops:
  7.2 9.2 %copy-start.1 = (bf16[256,2048]{1,0:T(8,128)(2,1)S(1)}, bf16[256,2048]{1,0:T(8,128)(2,1)}, u32[]{:S(2)}) copy-start(bf16[256,2048]{1,0:T(8,128)(2,1)} %param.7) | copy-start | bytes 3145732
  7.2 66.6 %all-gather.3.cloned.1.call-start = ((), (), s32[]{:S(2)}) async-start(), calls=%async_computation.3 | async-start | bytes 4325376 | tf_op jit(solution)/shard_map/all_gather | solution.py:137
  14.4 110.2 %all-gather.5.cloned.1.call-start = ((), (), s32[]{:S(2)}) async-start(), calls=%async_computation.4 | async-start | bytes 4325376 | tf_op jit(solution)/shard_map/all_gather | solution.py:138
  19.5 0.5 copy-start.5
  22.5 25.9 %all-to-all-start = ((bf16[32,8,2048]{2,1,0:T(8,128)(2,1)}), bf16[32,8,2048]{2,1,0:T(8,128)(2,1)S(1)}, u32[]{:S(2)}, u32[]{:S(2)}) async-start(bf16[32,8,2048]{2,1,0:T(8,128)(2,1)} %broadcast_select_fusion), calls=%async_computation | async-start | bytes 2097152 | tf_op jit(solution)/shard_map/all_to_all | solution.py:119
  134.3 4.6 copy-start.2
  134.3 5.9 %copy-start = (f32[2,512,256,8]{2,1,3,0:T(8,128)S(1)}, f32[2,512,256,8]{2,1,3,0:T(8,128)}, u32[]{:S(2)}) copy-start(f32[2,512,256,8]{2,1,3,0:T(8,128)} %get-tuple-element.409) | copy-start | bytes 25165828 | tf_op jit(solution)/shard_map/while
  138.9 4.7 copy-start.3
  153.3 4.6 copy-start.2
  153.3 5.9 %copy-start = (f32[2,512,256,8]{2,1,3,0:T(8,128)S(1)}, f32[2,512,256,8]{2,1,3,0:T(8,128)}, u32[]{:S(2)}) copy-start(f32[2,512,256,8]{2,1,3,0:T(8,128)} %get-tuple-element.409) | copy-start | bytes 25165828 | tf_op jit(solution)/shard_map/while
  157.9 4.7 copy-start.3
  172.4 4.6 copy-start.2
  172.4 5.9 %copy-start = (f32[2,512,256,8]{2,1,3,0:T(8,128)S(1)}, f32[2,512,256,8]{2,1,3,0:T(8,128)}, u32[]{:S(2)}) copy-start(f32[2,512,256,8]{2,1,3,0:T(8,128)} %get-tuple-element.409) | copy-start | bytes 25165828 | tf_op jit(solution)/shard_map/while
  177.0 4.7 copy-start.3
  191.4 4.6 copy-start.2
  191.4 5.9 %copy-start = (f32[2,512,256,8]{2,1,3,0:T(8,128)S(1)}, f32[2,512,256,8]{2,1,3,0:T(8,128)}, u32[]{:S(2)}) copy-start(f32[2,512,256,8]{2,1,3,0:T(8,128)} %get-tuple-element.409) | copy-start | bytes 25165828 | tf_op jit(solution)/shard_map/while
  196.0 4.7 copy-start.3
  210.4 4.6 copy-start.2
  210.4 5.9 %copy-start = (f32[2,512,256,8]{2,1,3,0:T(8,128)S(1)}, f32[2,512,256,8]{2,1,3,0:T(8,128)}, u32[]{:S(2)}) copy-start(f32[2,512,256,8]{2,1,3,0:T(8,128)} %get-tuple-element.409) | copy-start | bytes 25165828 | tf_op jit(solution)/shard_map/while
  215.1 4.7 copy-start.3
  229.5 4.6 copy-start.2
  229.5 5.9 %copy-start = (f32[2,512,256,8]{2,1,3,0:T(8,128)S(1)}, f32[2,512,256,8]{2,1,3,0:T(8,128)}, u32[]{:S(2)}) copy-start(f32[2,512,256,8]{2,1,3,0:T(8,128)} %get-tuple-element.409) | copy-start | bytes 25165828 | tf_op jit(solution)/shard_map/while
  234.1 4.7 copy-start.3
  248.5 4.6 copy-start.2
  248.5 5.9 %copy-start = (f32[2,512,256,8]{2,1,3,0:T(8,128)S(1)}, f32[2,512,256,8]{2,1,3,0:T(8,128)}, u32[]{:S(2)}) copy-start(f32[2,512,256,8]{2,1,3,0:T(8,128)} %get-tuple-element.409) | copy-start | bytes 25165828 | tf_op jit(solution)/shard_map/while
  253.1 4.7 copy-start.3
  267.6 4.6 copy-start.2
  267.6 5.9 %copy-start = (f32[2,512,256,8]{2,1,3,0:T(8,128)S(1)}, f32[2,512,256,8]{2,1,3,0:T(8,128)}, u32[]{:S(2)}) copy-start(f32[2,512,256,8]{2,1,3,0:T(8,128)} %get-tuple-element.409) | copy-start | bytes 25165828 | tf_op jit(solution)/shard_map/while
  272.2 4.7 copy-start.3
  286.6 4.6 copy-start.2
  286.6 5.9 %copy-start = (f32[2,512,256,8]{2,1,3,0:T(8,128)S(1)}, f32[2,512,256,8]{2,1,3,0:T(8,128)}, u32[]{:S(2)}) copy-start(f32[2,512,256,8]{2,1,3,0:T(8,128)} %get-tuple-element.409) | copy-start | bytes 25165828 | tf_op jit(solution)/shard_map/while
  291.2 4.7 copy-start.3
  305.6 4.6 copy-start.2
  305.6 5.9 %copy-start = (f32[2,512,256,8]{2,1,3,0:T(8,128)S(1)}, f32[2,512,256,8]{2,1,3,0:T(8,128)}, u32[]{:S(2)}) copy-start(f32[2,512,256,8]{2,1,3,0:T(8,128)} %get-tuple-element.409) | copy-start | bytes 25165828 | tf_op jit(solution)/shard_map/while
  310.3 4.7 copy-start.3
  324.7 4.6 copy-start.2
  324.7 5.9 %copy-start = (f32[2,512,256,8]{2,1,3,0:T(8,128)S(1)}, f32[2,512,256,8]{2,1,3,0:T(8,128)}, u32[]{:S(2)}) copy-start(f32[2,512,256,8]{2,1,3,0:T(8,128)} %get-tuple-element.409) | copy-start | bytes 25165828 | tf_op jit(solution)/shard_map/while
  329.3 4.7 copy-start.3
  343.7 4.6 copy-start.2
  343.7 5.9 %copy-start = (f32[2,512,256,8]{2,1,3,0:T(8,128)S(1)}, f32[2,512,256,8]{2,1,3,0:T(8,128)}, u32[]{:S(2)}) copy-start(f32[2,512,256,8]{2,1,3,0:T(8,128)} %get-tuple-element.409) | copy-start | bytes 25165828 | tf_op jit(solution)/shard_map/while
  348.3 4.7 copy-start.3
  362.8 4.6 copy-start.2
  362.8 5.9 %copy-start = (f32[2,512,256,8]{2,1,3,0:T(8,128)S(1)}, f32[2,512,256,8]{2,1,3,0:T(8,128)}, u32[]{:S(2)}) copy-start(f32[2,512,256,8]{2,1,3,0:T(8,128)} %get-tuple-element.409) | copy-start | bytes 25165828 | tf_op jit(solution)/shard_map/while
  367.4 4.7 copy-start.3
  381.8 4.6 copy-start.2
  381.8 5.9 %copy-start = (f32[2,512,256,8]{2,1,3,0:T(8,128)S(1)}, f32[2,512,256,8]{2,1,3,0:T(8,128)}, u32[]{:S(2)}) copy-start(f32[2,512,256,8]{2,1,3,0:T(8,128)} %get-tuple-element.409) | copy-start | bytes 25165828 | tf_op jit(solution)/shard_map/while
  386.4 4.7 copy-start.3
  400.8 4.6 copy-start.2
  400.8 5.9 %copy-start = (f32[2,512,256,8]{2,1,3,0:T(8,128)S(1)}, f32[2,512,256,8]{2,1,3,0:T(8,128)}, u32[]{:S(2)}) copy-start(f32[2,512,256,8]{2,1,3,0:T(8,128)} %get-tuple-element.409) | copy-start | bytes 25165828 | tf_op jit(solution)/shard_map/while
  405.5 4.7 copy-start.3
  419.9 4.6 copy-start.2
  419.9 5.9 %copy-start = (f32[2,512,256,8]{2,1,3,0:T(8,128)S(1)}, f32[2,512,256,8]{2,1,3,0:T(8,128)}, u32[]{:S(2)}) copy-start(f32[2,512,256,8]{2,1,3,0:T(8,128)} %get-tuple-element.409) | copy-start | bytes 25165828 | tf_op jit(solution)/shard_map/while
  424.5 4.7 copy-start.3
  431.9 23.6 %copy-start.6 = (s32[32]{0:T(128)S(1)}, s32[32]{0:T(128)}, u32[]{:S(2)}) copy-start(s32[32]{0:T(128)} %copy-done.5) | copy-start | bytes 388
  455.5 9.0 %copy-start.4 = (f32[2,8,256]{2,1,0:T(8,128)S(1)}, f32[2,8,256]{2,1,0:T(8,128)}, u32[]{:S(2)}) copy-start(f32[2,8,256]{2,1,0:T(8,128)} %get-tuple-element.238) | copy-start | bytes 49156
  460.1 19.8 %all-to-all-start.2 = ((bf16[4,64,2048]{2,1,0:T(8,128)(2,1)}), bf16[4,64,2048]{2,1,0:T(8,128)(2,1)S(1)}, u32[]{:S(2)}, u32[]{:S(2)}) async-start(bf16[4,64,2048]{2,1,0:T(8,128)(2,1)} %bitcast.7), calls=%async_computation.2 | async-start | bytes 2097152 | tf_op jit(solution)/shard_map/all_to_all | solution.py:153
Sparse Core Ops, SparseCore 0:
  14.5 59.1 all-gather.2
  75.9 48.6 all-gather.4
where the time goes:
time: 490 us; the launch traced here: 488 us
  matrix products  141 us (29%)
  other arithmetic  136 us (28%)
  waiting for transfers between devices  109 us (22%)
  local copies, waits for them, and re-layouts  51.6 us (11%)
  blocking collectives  22.5 us (5%)
  between operations  14.2 us (3%)
  starting transfers between devices  12.1 us (2%)
    dot_general x16, matrix products, attend_block(): jnp.einsum('rgqd,ngd->gqrn', query_rows, key_rows, preferred_element_type...  85.4 us
    reduce_sum x16, other arithmetic, attend_block(): row_sum = row_sum * factor + jnp.sum(weights, axis=-1)  73.4 us
    dot_general x16, matrix products, attend_block(): jnp.einsum('gqrn,ngd->gqrd', probs, value_rows, preferred_element_type=jn...  55.7 us
    all_gather x1, waiting for transfers between devices, body(): lax.all_gather(value_states, 'tok', axis=0, tiled=True)  50.9 us
    all_gather x1, waiting for transfers between devices, body(): lax.all_gather(k_rot, 'tok', axis=0, tiled=True)  24.8 us
    all_to_all x1, blocking collectives, body(): lax.all_to_all(result.reshape(shards, block_rows, q_local * HEAD_DIM), 't...  22.5 us
    while x112, local copies, waits for them, and re-layouts  19.7 us
    all_to_all x1, waiting for transfers between devices, body(): lax.all_to_all(outgoing, 'tok', split_axis=0, concat_axis=0, tiled=True)  18.3 us
  transfers between devices with their start and end apart: 4, of which 4 were waited for; matrix products, arithmetic and copies ran while one was open for 2% of the time, Pallas kernels for 0%

commit v1 on v0

--- a/solution.py
+++ b/solution.py
@@ -134,7 +134,9 @@
     final_state = folder(
         initial,
         (
-            lax.all_gather(k_rot, "tok", axis=0, tiled=True),
+            jnp.concatenate(
+                lax.all_to_all(jnp.stack([k_rot] * lax.axis_size("tok")), "tok", 0, 0), axis=0
+            ),
             lax.all_gather(value_states, "tok", axis=0, tiled=True),
         ),
         jnp.int32(0),

time: 490 us -> 507 us (1.035)
  local copies, waits for them, and re-layouts: 51.6 us -> 81.1 us
  waiting for transfers between devices: 109 us -> 87.6 us
  starting transfers between devices: 12.1 us -> 18.2 us
    all_to_all x0 -> x1, waiting for transfers between devices: none -> 56.7 us  [body(): lax.all_to_all(jnp.stack([k_rot] * lax.axis_size('tok')), 'tok', 0, 0)]
    all_gather x1, waiting for transfers between devices: 50.9 us -> 0.01 us  [body(): lax.all_gather(value_states, 'tok', axis=0, tiled=True)]
    all_gather x1 -> x0, waiting for transfers between devices: 24.8 us -> none  [body(): lax.all_gather(k_rot, 'tok', axis=0, tiled=True)]
    dynamic_slice x0 -> x32, local copies, waits for them, and re-layouts: none -> 17.8 us  [inner(): lax.dynamic_slice_in_dim(key_piece, offset, stride, 0)]
    all_to_all x0 -> x1, local copies, waits for them, and re-layouts: none -> 6.49 us  [body(): lax.all_to_all(jnp.stack([k_rot] * lax.axis_size('tok')), 'tok', 0, 0)]
    while x112 -> x176, local copies, waits for them, and re-layouts: 19.7 us -> 21.4 us
  transfers between devices with their start and end apart: 4 -> 4, of which waited for: 4 -> 3; matrix products, arithmetic and copies ran while one was open for 2% -> 5% of each run, Pallas kernels for 0% -> 0%
where the time goes in v1:
time: 507 us; the launch traced here: 505 us
  matrix products  143 us (28%)
  other arithmetic  138 us (27%)
  waiting for transfers between devices  87.6 us (17%)
  local copies, waits for them, and re-layouts  81.1 us (16%)
  blocking collectives  21.1 us (4%)
  starting transfers between devices  18.2 us (4%)
  between operations  14.2 us (3%)
    dot_general x16, matrix products, attend_block(): jnp.einsum('rgqd,ngd->gqrn', query_rows, key_rows, preferred_element_type...  87.2 us
    reduce_sum x16, other arithmetic, attend_block(): row_sum = row_sum * factor + jnp.sum(weights, axis=-1)  73.4 us
    all_to_all x1, waiting for transfers between devices, body(): lax.all_to_all(jnp.stack([k_rot] * lax.axis_size('tok')), 'tok', 0, 0)  56.7 us
    dot_general x16, matrix products, attend_block(): jnp.einsum('gqrn,ngd->gqrd', probs, value_rows, preferred_element_type=jn...  55.7 us
    while x176, local copies, waits for them, and re-layouts  21.4 us
    all_to_all x1, blocking collectives, body(): lax.all_to_all(result.reshape(shards, block_rows, q_local * HEAD_DIM), 't...  21.1 us
    dynamic_slice x16, local copies, waits for them, and re-layouts, inner(): lax.dynamic_slice_in_dim(value_piece, offset, stride, 0)  19 us
    dynamic_slice x32, local copies, waits for them, and re-layouts, inner(): lax.dynamic_slice_in_dim(key_piece, offset, stride, 0)  17.8 us
  transfers between devices with their start and end apart: 4, of which 3 were waited for; matrix products, arithmetic and copies ran while one was open for 5% of the time, Pallas kernels for 0%

profile of v1, /device:TPU:0, one launch (start us, length us, event | category | flops | bytes accessed | tf_op | source)
XLA Modules:
  0.0 504.6 jit_solution(4118121220097687441)
XLA Ops:
  7.2 1.7 copy.46
  8.9 1.4 add_reduce_fusion
  11.1 1.4 broadcast_in_dim.111
  12.5 1.5 convert_bitcast_fusion
  21.9 7.4 %all-to-all-start.1 = ((bf16[32,8,2048]{2,1,0:T(8,128)(2,1)}), bf16[32,8,2048]{2,1,0:T(8,128)(2,1)S(1)}, u32[]{:S(2)}, u32[]{:S(2)}) async-start(bf16[32,8,2048]{2,1,0:T(8,128)(2,1)} %broadcast_select_fusion), calls=%async_computation.1 | async-start | bytes 2097152 | tf_op jit(solution)/shard_map/all_to_all | solution.py:119
  30.4 16.2 %all-to-all-done.1 = bf16[32,8,2048]{2,1,0:T(8,128)(2,1)S(1)} async-done(((bf16[32,8,2048]{2,1,0:T(8,128)(2,1)}), bf16[32,8,2048]{2,1,0:T(8,128)(2,1)S(1)}, u32[]{:S(2)}, u32[]{:S(2)}) %all-to-all-start.1) | async-done | bytes 1048608 | tf_op jit(solution)/shard_map/all_to_all | solution.py:119
  46.6 2.5 stack.2
  49.1 5.1 %all-to-all-start = ((bf16[32,256,256]{1,2,0:T(8,128)(2,1)}), bf16[32,256,256]{1,2,0:T(8,128)(2,1)}, u32[]{:S(2)}, u32[]{:S(2)}) async-start(bf16[32,256,256]{1,2,0:T(8,128)(2,1)} %stack.2), calls=%async_computation | async-start | bytes 8388608 | tf_op jit(solution)/shard_map/all_to_all | solution.py:138
  54.7 56.7 %all-to-all-done = bf16[32,256,256]{1,2,0:T(8,128)(2,1)} async-done(((bf16[32,256,256]{1,2,0:T(8,128)(2,1)}), bf16[32,256,256]{1,2,0:T(8,128)(2,1)}, u32[]{:S(2)}, u32[]{:S(2)}) %all-to-all-start) | async-done | bytes 4194336 | tf_op jit(solution)/shard_map/all_to_all | solution.py:138
  111.4 6.5 %copy.45 = bf16[32,256,256]{2,1,0:T(8,128)(2,1)} copy(bf16[32,256,256]{1,2,0:T(8,128)(2,1)} %all-to-all-done) | data formatting | bytes 8388608 | tf_op jit(solution)/shard_map/all_to_all | solution.py:138
  117.9 327.8 %while.20 = (s32[]{:T(128)}, f32[2,8,256]{2,1,0:T(8,128)S(1)}, f32[2,8,256]{2,1,0:T(8,128)}, f32[2,8,256,128]{3,2,1,0:T(8,128)}, s32[256]{0:T(256)}, /*index=5*/...) while((s32[]{:T(128)}, f32[2,8,256]{2,1,0:T(8,128)S(1)}, ...), condition=%wide.region_7.8_spmd.clone, body=%wide.region_3.7_spmd.clone.sunk | while | flops 1103148288 | bytes 83771936 | solution.py:86
  121.5 5.4 %fusion.32 = (f32[2,8,256]{2,1,0:T(8,128)}, f32[2,512,256,8]{2,1,3,0:T(8,128)}) fusion(pred[256,512]{0,1:T(8,128)(4,1)S(1)} %and_and_fusion.2, bf16[512,2,128,1]{0,2,3,1:T(8,128)(2,1)S(1)} %bitcast.72, bf16[256,2,8,128]{3,0,2,1:T(8,128)(2,1)S(1)} %get-tuple-element.462), kind=kOutput, calls=%fused_computation.5.clone.1 | convolution fusion | flops 543158272 | bytes 9846784 | tf_op jit(solution)/shard_map/while/body/eval_jaxpr/rgqd,ngd->gqrn/dot_general | solution.py:44
  127.7 4.6 fusion.33
  133.6 3.5 fusion.35
  142.0 5.4 %fusion.32 = (f32[2,8,256]{2,1,0:T(8,128)}, f32[2,512,256,8]{2,1,3,0:T(8,128)}) fusion(pred[256,512]{0,1:T(8,128)(4,1)S(1)} %and_and_fusion.2, bf16[512,2,128,1]{0,2,3,1:T(8,128)(2,1)S(1)} %bitcast.72, bf16[256,2,8,128]{3,0,2,1:T(8,128)(2,1)S(1)} %get-tuple-element.462), kind=kOutput, calls=%fused_computation.5.clone.1 | convolution fusion | flops 543158272 | bytes 9846784 | tf_op jit(solution)/shard_map/while/body/eval_jaxpr/rgqd,ngd->gqrn/dot_general | solution.py:44
  148.2 4.6 fusion.33
  154.0 3.5 fusion.35
  162.5 5.4 %fusion.32 = (f32[2,8,256]{2,1,0:T(8,128)}, f32[2,512,256,8]{2,1,3,0:T(8,128)}) fusion(pred[256,512]{0,1:T(8,128)(4,1)S(1)} %and_and_fusion.2, bf16[512,2,128,1]{0,2,3,1:T(8,128)(2,1)S(1)} %bitcast.72, bf16[256,2,8,128]{3,0,2,1:T(8,128)(2,1)S(1)} %get-tuple-element.462), kind=kOutput, calls=%fused_computation.5.clone.1 | convolution fusion | flops 543158272 | bytes 9846784 | tf_op jit(solution)/shard_map/while/body/eval_jaxpr/rgqd,ngd->gqrn/dot_general | solution.py:44
  168.7 4.6 fusion.33
  174.5 3.5 fusion.35
  183.0 5.4 %fusion.32 = (f32[2,8,256]{2,1,0:T(8,128)}, f32[2,512,256,8]{2,1,3,0:T(8,128)}) fusion(pred[256,512]{0,1:T(8,128)(4,1)S(1)} %and_and_fusion.2, bf16[512,2,128,1]{0,2,3,1:T(8,128)(2,1)S(1)} %bitcast.72, bf16[256,2,8,128]{3,0,2,1:T(8,128)(2,1)S(1)} %get-tuple-element.462), kind=kOutput, calls=%fused_computation.5.clone.1 | convolution fusion | flops 543158272 | bytes 9846784 | tf_op jit(solution)/shard_map/while/body/eval_jaxpr/rgqd,ngd->gqrn/dot_general | solution.py:44
  189.2 4.6 fusion.33
  195.0 3.5 fusion.35
  203.5 5.4 %fusion.32 = (f32[2,8,256]{2,1,0:T(8,128)}, f32[2,512,256,8]{2,1,3,0:T(8,128)}) fusion(pred[256,512]{0,1:T(8,128)(4,1)S(1)} %and_and_fusion.2, bf16[512,2,128,1]{0,2,3,1:T(8,128)(2,1)S(1)} %bitcast.72, bf16[256,2,8,128]{3,0,2,1:T(8,128)(2,1)S(1)} %get-tuple-element.462), kind=kOutput, calls=%fused_computation.5.clone.1 | convolution fusion | flops 543158272 | bytes 9846784 | tf_op jit(solution)/shard_map/while/body/eval_jaxpr/rgqd,ngd->gqrn/dot_general | solution.py:44
  209.7 4.6 fusion.33
  215.5 3.5 fusion.35
  224.0 5.4 %fusion.32 = (f32[2,8,256]{2,1,0:T(8,128)}, f32[2,512,256,8]{2,1,3,0:T(8,128)}) fusion(pred[256,512]{0,1:T(8,128)(4,1)S(1)} %and_and_fusion.2, bf16[512,2,128,1]{0,2,3,1:T(8,128)(2,1)S(1)} %bitcast.72, bf16[256,2,8,128]{3,0,2,1:T(8,128)(2,1)S(1)} %get-tuple-element.462), kind=kOutput, calls=%fused_computation.5.clone.1 | convolution fusion | flops 543158272 | bytes 9846784 | tf_op jit(solution)/shard_map/while/body/eval_jaxpr/rgqd,ngd->gqrn/dot_general | solution.py:44
  230.1 4.6 fusion.33
  236.0 3.5 fusion.35
  244.5 5.4 %fusion.32 = (f32[2,8,256]{2,1,0:T(8,128)}, f32[2,512,256,8]{2,1,3,0:T(8,128)}) fusion(pred[256,512]{0,1:T(8,128)(4,1)S(1)} %and_and_fusion.2, bf16[512,2,128,1]{0,2,3,1:T(8,128)(2,1)S(1)} %bitcast.72, bf16[256,2,8,128]{3,0,2,1:T(8,128)(2,1)S(1)} %get-tuple-element.462), kind=kOutput, calls=%fused_computation.5.clone.1 | convolution fusion | flops 543158272 | bytes 9846784 | tf_op jit(solution)/shard_map/while/body/eval_jaxpr/rgqd,ngd->gqrn/dot_general | solution.py:44
  250.6 4.6 fusion.33
  256.5 3.5 fusion.35
  265.0 5.4 %fusion.32 = (f32[2,8,256]{2,1,0:T(8,128)}, f32[2,512,256,8]{2,1,3,0:T(8,128)}) fusion(pred[256,512]{0,1:T(8,128)(4,1)S(1)} %and_and_fusion.2, bf16[512,2,128,1]{0,2,3,1:T(8,128)(2,1)S(1)} %bitcast.72, bf16[256,2,8,128]{3,0,2,1:T(8,128)(2,1)S(1)} %get-tuple-element.462), kind=kOutput, calls=%fused_computation.5.clone.1 | convolution fusion | flops 543158272 | bytes 9846784 | tf_op jit(solution)/shard_map/while/body/eval_jaxpr/rgqd,ngd->gqrn/dot_general | solution.py:44
  271.1 4.6 fusion.33
  277.0 3.5 fusion.35
  285.4 5.4 %fusion.32 = (f32[2,8,256]{2,1,0:T(8,128)}, f32[2,512,256,8]{2,1,3,0:T(8,128)}) fusion(pred[256,512]{0,1:T(8,128)(4,1)S(1)} %and_and_fusion.2, bf16[512,2,128,1]{0,2,3,1:T(8,128)(2,1)S(1)} %bitcast.72, bf16[256,2,8,128]{3,0,2,1:T(8,128)(2,1)S(1)} %get-tuple-element.462), kind=kOutput, calls=%fused_computation.5.clone.1 | convolution fusion | flops 543158272 | bytes 9846784 | tf_op jit(solution)/shard_map/while/body/eval_jaxpr/rgqd,ngd->gqrn/dot_general | solution.py:44
  291.6 4.6 fusion.33
  297.5 3.5 fusion.35
  305.9 5.4 %fusion.32 = (f32[2,8,256]{2,1,0:T(8,128)}, f32[2,512,256,8]{2,1,3,0:T(8,128)}) fusion(pred[256,512]{0,1:T(8,128)(4,1)S(1)} %and_and_fusion.2, bf16[512,2,128,1]{0,2,3,1:T(8,128)(2,1)S(1)} %bitcast.72, bf16[256,2,8,128]{3,0,2,1:T(8,128)(2,1)S(1)} %get-tuple-element.462), kind=kOutput, calls=%fused_computation.5.clone.1 | convolution fusion | flops 543158272 | bytes 9846784 | tf_op jit(solution)/shard_map/while/body/eval_jaxpr/rgqd,ngd->gqrn/dot_general | solution.py:44
  312.1 4.6 fusion.33
  318.0 3.5 fusion.35
  326.4 5.4 %fusion.32 = (f32[2,8,256]{2,1,0:T(8,128)}, f32[2,512,256,8]{2,1,3,0:T(8,128)}) fusion(pred[256,512]{0,1:T(8,128)(4,1)S(1)} %and_and_fusion.2, bf16[512,2,128,1]{0,2,3,1:T(8,128)(2,1)S(1)} %bitcast.72, bf16[256,2,8,128]{3,0,2,1:T(8,128)(2,1)S(1)} %get-tuple-element.462), kind=kOutput, calls=%fused_computation.5.clone.1 | convolution fusion | flops 543158272 | bytes 9846784 | tf_op jit(solution)/shard_map/while/body/eval_jaxpr/rgqd,ngd->gqrn/dot_general | solution.py:44
  332.6 4.6 fusion.33
  338.5 3.5 fusion.35
  346.9 5.4 %fusion.32 = (f32[2,8,256]{2,1,0:T(8,128)}, f32[2,512,256,8]{2,1,3,0:T(8,128)}) fusion(pred[256,512]{0,1:T(8,128)(4,1)S(1)} %and_and_fusion.2, bf16[512,2,128,1]{0,2,3,1:T(8,128)(2,1)S(1)} %bitcast.72, bf16[256,2,8,128]{3,0,2,1:T(8,128)(2,1)S(1)} %get-tuple-element.462), kind=kOutput, calls=%fused_computation.5.clone.1 | convolution fusion | flops 543158272 | bytes 9846784 | tf_op jit(solution)/shard_map/while/body/eval_jaxpr/rgqd,ngd->gqrn/dot_general | solution.py:44
  353.1 4.6 fusion.33
  358.9 3.5 fusion.35
  367.4 5.4 %fusion.32 = (f32[2,8,256]{2,1,0:T(8,128)}, f32[2,512,256,8]{2,1,3,0:T(8,128)}) fusion(pred[256,512]{0,1:T(8,128)(4,1)S(1)} %and_and_fusion.2, bf16[512,2,128,1]{0,2,3,1:T(8,128)(2,1)S(1)} %bitcast.72, bf16[256,2,8,128]{3,0,2,1:T(8,128)(2,1)S(1)} %get-tuple-element.462), kind=kOutput, calls=%fused_computation.5.clone.1 | convolution fusion | flops 543158272 | bytes 9846784 | tf_op jit(solution)/shard_map/while/body/eval_jaxpr/rgqd,ngd->gqrn/dot_general | solution.py:44
  373.6 4.6 fusion.33
  379.4 3.5 fusion.35
  387.9 5.4 %fusion.32 = (f32[2,8,256]{2,1,0:T(8,128)}, f32[2,512,256,8]{2,1,3,0:T(8,128)}) fusion(pred[256,512]{0,1:T(8,128)(4,1)S(1)} %and_and_fusion.2, bf16[512,2,128,1]{0,2,3,1:T(8,128)(2,1)S(1)} %bitcast.72, bf16[256,2,8,128]{3,0,2,1:T(8,128)(2,1)S(1)} %get-tuple-element.462), kind=kOutput, calls=%fused_computation.5.clone.1 | convolution fusion | flops 543158272 | bytes 9846784 | tf_op jit(solution)/shard_map/while/body/eval_jaxpr/rgqd,ngd->gqrn/dot_general | solution.py:44
  394.1 4.6 fusion.33
  399.9 3.5 fusion.35
  408.4 5.4 %fusion.32 = (f32[2,8,256]{2,1,0:T(8,128)}, f32[2,512,256,8]{2,1,3,0:T(8,128)}) fusion(pred[256,512]{0,1:T(8,128)(4,1)S(1)} %and_and_fusion.2, bf16[512,2,128,1]{0,2,3,1:T(8,128)(2,1)S(1)} %bitcast.72, bf16[256,2,8,128]{3,0,2,1:T(8,128)(2,1)S(1)} %get-tuple-element.462), kind=kOutput, calls=%fused_computation.5.clone.1 | convolution fusion | flops 543158272 | bytes 9846784 | tf_op jit(solution)/shard_map/while/body/eval_jaxpr/rgqd,ngd->gqrn/dot_general | solution.py:44
  414.6 4.6 fusion.33
  420.4 3.5 fusion.35
  428.9 5.4 %fusion.32 = (f32[2,8,256]{2,1,0:T(8,128)}, f32[2,512,256,8]{2,1,3,0:T(8,128)}) fusion(pred[256,512]{0,1:T(8,128)(4,1)S(1)} %and_and_fusion.2, bf16[512,2,128,1]{0,2,3,1:T(8,128)(2,1)S(1)} %bitcast.72, bf16[256,2,8,128]{3,0,2,1:T(8,128)(2,1)S(1)} %get-tuple-element.462), kind=kOutput, calls=%fused_computation.5.clone.1 | convolution fusion | flops 543158272 | bytes 9846784 | tf_op jit(solution)/shard_map/while/body/eval_jaxpr/rgqd,ngd->gqrn/dot_general | solution.py:44
  435.0 4.6 fusion.33
  440.9 3.5 fusion.35
  445.7 2.0 fusion.15
  448.9 21.1 %all_to_all.34 = bf16[32,8,2048]{2,1,0:T(8,128)(2,1)S(1)} all-to-all(bf16[32,8,2048]{2,1,0:T(8,128)(2,1)S(1)} %convert_element_type.58), channel_id=1, replica_groups=mesh['tok'=32,'kv'=4] {'tok'}, dimensions={0} | all-to-all | bytes 2097152 | tf_op jit(solution)/shard_map/all_to_all | solution.py:145
  471.1 4.6 scatter_fusion
  475.7 5.7 %all-to-all-start.3 = ((bf16[4,64,2048]{2,1,0:T(8,128)(2,1)}), bf16[4,64,2048]{2,1,0:T(8,128)(2,1)S(1)}, u32[]{:S(2)}, u32[]{:S(2)}) async-start(bf16[4,64,2048]{2,1,0:T(8,128)(2,1)} %bitcast.8), calls=%async_computation.3 | async-start | bytes 2097152 | tf_op jit(solution)/shard_map/all_to_all | solution.py:155
  482.0 14.8 %all-to-all-done.3 = bf16[4,64,2048]{2,1,0:T(8,128)(2,1)S(1)} async-done(((bf16[4,64,2048]{2,1,0:T(8,128)(2,1)}), bf16[4,64,2048]{2,1,0:T(8,128)(2,1)S(1)}, u32[]{:S(2)}, u32[]{:S(2)}) %all-to-all-start.3) | async-done | bytes 1048608 | tf_op jit(solution)/shard_map/all_to_all | solution.py:155
  (395 shorter events, 123.9 us)
Async XLA Ops:
  7.2 7.3 %copy-start.9 = (s32[16]{0:T(128)S(1)}, s32[16]{0:T(128)}, u32[]{:S(2)}) copy-start(s32[16]{0:T(128)} %param.10) | copy-start | bytes 196
  7.2 110.7 %all-gather.2.cloned.1.call-start = ((), (), s32[]{:S(2)}) async-start(), calls=%async_computation.4 | async-start | bytes 4325376 | tf_op jit(solution)/shard_map/all_gather | solution.py:140
  17.7 11.6 %copy-start.6 = (bf16[256,256]{1,0:T(8,128)(2,1)S(1)}, bf16[256,256]{1,0:T(8,128)(2,1)}, u32[]{:S(2)}) copy-start(bf16[256,256]{1,0:T(8,128)(2,1)} %param.8) | copy-start | bytes 393220
  21.9 24.7 %all-to-all-start.1 = ((bf16[32,8,2048]{2,1,0:T(8,128)(2,1)}), bf16[32,8,2048]{2,1,0:T(8,128)(2,1)S(1)}, u32[]{:S(2)}, u32[]{:S(2)}) async-start(bf16[32,8,2048]{2,1,0:T(8,128)(2,1)} %broadcast_select_fusion), calls=%async_computation.1 | async-start | bytes 2097152 | tf_op jit(solution)/shard_map/all_to_all | solution.py:119
  49.1 62.3 %all-to-all-start = ((bf16[32,256,256]{1,2,0:T(8,128)(2,1)}), bf16[32,256,256]{1,2,0:T(8,128)(2,1)}, u32[]{:S(2)}, u32[]{:S(2)}) async-start(bf16[32,256,256]{1,2,0:T(8,128)(2,1)} %stack.2), calls=%async_computation | async-start | bytes 8388608 | tf_op jit(solution)/shard_map/all_to_all | solution.py:138
  121.5 12.0 %copy-start.1 = (f32[2,8,256,128]{3,2,1,0:T(8,128)S(1)}, f32[2,8,256,128]{3,2,1,0:T(8,128)}, u32[]{:S(2)}) copy-start(f32[2,8,256,128]{3,2,1,0:T(8,128)} %get-tuple-element.444) | copy-start | bytes 6291460 | tf_op jit(solution)/shard_map/while
  127.7 4.6 copy-start.3
  127.7 5.9 %copy-start = (f32[2,512,256,8]{2,1,3,0:T(8,128)S(1)}, f32[2,512,256,8]{2,1,3,0:T(8,128)}, u32[]{:S(2)}) copy-start(f32[2,512,256,8]{2,1,3,0:T(8,128)} %get-tuple-element.424) | copy-start | bytes 25165828 | tf_op jit(solution)/shard_map/while
  132.3 4.7 copy-start.4
  142.0 12.0 %copy-start.1 = (f32[2,8,256,128]{3,2,1,0:T(8,128)S(1)}, f32[2,8,256,128]{3,2,1,0:T(8,128)}, u32[]{:S(2)}) copy-start(f32[2,8,256,128]{3,2,1,0:T(8,128)} %get-tuple-element.444) | copy-start | bytes 6291460 | tf_op jit(solution)/shard_map/while
  148.2 4.6 copy-start.3
  148.2 5.9 %copy-start = (f32[2,512,256,8]{2,1,3,0:T(8,128)S(1)}, f32[2,512,256,8]{2,1,3,0:T(8,128)}, u32[]{:S(2)}) copy-start(f32[2,512,256,8]{2,1,3,0:T(8,128)} %get-tuple-element.424) | copy-start | bytes 25165828 | tf_op jit(solution)/shard_map/while
  152.8 4.7 copy-start.4
  162.5 12.0 %copy-start.1 = (f32[2,8,256,128]{3,2,1,0:T(8,128)S(1)}, f32[2,8,256,128]{3,2,1,0:T(8,128)}, u32[]{:S(2)}) copy-start(f32[2,8,256,128]{3,2,1,0:T(8,128)} %get-tuple-element.444) | copy-start | bytes 6291460 | tf_op jit(solution)/shard_map/while
  168.7 4.6 copy-start.3
  168.7 5.9 %copy-start = (f32[2,512,256,8]{2,1,3,0:T(8,128)S(1)}, f32[2,512,256,8]{2,1,3,0:T(8,128)}, u32[]{:S(2)}) copy-start(f32[2,512,256,8]{2,1,3,0:T(8,128)} %get-tuple-element.424) | copy-start | bytes 25165828 | tf_op jit(solution)/shard_map/while
  173.3 4.7 copy-start.4
  183.0 12.0 %copy-start.1 = (f32[2,8,256,128]{3,2,1,0:T(8,128)S(1)}, f32[2,8,256,128]{3,2,1,0:T(8,128)}, u32[]{:S(2)}) copy-start(f32[2,8,256,128]{3,2,1,0:T(8,128)} %get-tuple-element.444) | copy-start | bytes 6291460 | tf_op jit(solution)/shard_map/while
  189.2 4.6 copy-start.3
  189.2 5.9 %copy-start = (f32[2,512,256,8]{2,1,3,0:T(8,128)S(1)}, f32[2,512,256,8]{2,1,3,0:T(8,128)}, u32[]{:S(2)}) copy-start(f32[2,512,256,8]{2,1,3,0:T(8,128)} %get-tuple-element.424) | copy-start | bytes 25165828 | tf_op jit(solution)/shard_map/while
  193.8 4.7 copy-start.4
  203.5 12.0 %copy-start.1 = (f32[2,8,256,128]{3,2,1,0:T(8,128)S(1)}, f32[2,8,256,128]{3,2,1,0:T(8,128)}, u32[]{:S(2)}) copy-start(f32[2,8,256,128]{3,2,1,0:T(8,128)} %get-tuple-element.444) | copy-start | bytes 6291460 | tf_op jit(solution)/shard_map/while
  209.7 4.6 copy-start.3
  209.7 5.9 %copy-start = (f32[2,512,256,8]{2,1,3,0:T(8,128)S(1)}, f32[2,512,256,8]{2,1,3,0:T(8,128)}, u32[]{:S(2)}) copy-start(f32[2,512,256,8]{2,1,3,0:T(8,128)} %get-tuple-element.424) | copy-start | bytes 25165828 | tf_op jit(solution)/shard_map/while
  214.3 4.7 copy-start.4
  224.0 12.0 %copy-start.1 = (f32[2,8,256,128]{3,2,1,0:T(8,128)S(1)}, f32[2,8,256,128]{3,2,1,0:T(8,128)}, u32[]{:S(2)}) copy-start(f32[2,8,256,128]{3,2,1,0:T(8,128)} %get-tuple-element.444) | copy-start | bytes 6291460 | tf_op jit(solution)/shard_map/while
  230.1 4.6 copy-start.3
  230.1 5.9 %copy-start = (f32[2,512,256,8]{2,1,3,0:T(8,128)S(1)}, f32[2,512,256,8]{2,1,3,0:T(8,128)}, u32[]{:S(2)}) copy-start(f32[2,512,256,8]{2,1,3,0:T(8,128)} %get-tuple-element.424) | copy-start | bytes 25165828 | tf_op jit(solution)/shard_map/while
  234.8 4.7 copy-start.4
  244.5 12.0 %copy-start.1 = (f32[2,8,256,128]{3,2,1,0:T(8,128)S(1)}, f32[2,8,256,128]{3,2,1,0:T(8,128)}, u32[]{:S(2)}) copy-start(f32[2,8,256,128]{3,2,1,0:T(8,128)} %get-tuple-element.444) | copy-start | bytes 6291460 | tf_op jit(solution)/shard_map/while
  250.6 5.9 %copy-start = (f32[2,512,256,8]{2,1,3,0:T(8,128)S(1)}, f32[2,512,256,8]{2,1,3,0:T(8,128)}, u32[]{:S(2)}) copy-start(f32[2,512,256,8]{2,1,3,0:T(8,128)} %get-tuple-element.424) | copy-start | bytes 25165828 | tf_op jit(solution)/shard_map/while
  255.3 4.7 copy-start.4
  264.9 12.0 %copy-start.1 = (f32[2,8,256,128]{3,2,1,0:T(8,128)S(1)}, f32[2,8,256,128]{3,2,1,0:T(8,128)}, u32[]{:S(2)}) copy-start(f32[2,8,256,128]{3,2,1,0:T(8,128)} %get-tuple-element.444) | copy-start | bytes 6291460 | tf_op jit(solution)/shard_map/while
  271.1 4.6 copy-start.3
  271.1 5.9 %copy-start = (f32[2,512,256,8]{2,1,3,0:T(8,128)S(1)}, f32[2,512,256,8]{2,1,3,0:T(8,128)}, u32[]{:S(2)}) copy-start(f32[2,512,256,8]{2,1,3,0:T(8,128)} %get-tuple-element.424) | copy-start | bytes 25165828 | tf_op jit(solution)/shard_map/while
  275.8 4.7 copy-start.4
  285.4 12.0 %copy-start.1 = (f32[2,8,256,128]{3,2,1,0:T(8,128)S(1)}, f32[2,8,256,128]{3,2,1,0:T(8,128)}, u32[]{:S(2)}) copy-start(f32[2,8,256,128]{3,2,1,0:T(8,128)} %get-tuple-element.444) | copy-start | bytes 6291460 | tf_op jit(solution)/shard_map/while
  291.6 5.9 %copy-start = (f32[2,512,256,8]{2,1,3,0:T(8,128)S(1)}, f32[2,512,256,8]{2,1,3,0:T(8,128)}, u32[]{:S(2)}) copy-start(f32[2,512,256,8]{2,1,3,0:T(8,128)} %get-tuple-element.424) | copy-start | bytes 25165828 | tf_op jit(solution)/shard_map/while
  296.2 4.7 copy-start.4
  305.9 12.0 %copy-start.1 = (f32[2,8,256,128]{3,2,1,0:T(8,128)S(1)}, f32[2,8,256,128]{3,2,1,0:T(8,128)}, u32[]{:S(2)}) copy-start(f32[2,8,256,128]{3,2,1,0:T(8,128)} %get-tuple-element.444) | copy-start | bytes 6291460 | tf_op jit(solution)/shard_map/while
  312.1 5.9 %copy-start = (f32[2,512,256,8]{2,1,3,0:T(8,128)S(1)}, f32[2,512,256,8]{2,1,3,0:T(8,128)}, u32[]{:S(2)}) copy-start(f32[2,512,256,8]{2,1,3,0:T(8,128)} %get-tuple-element.424) | copy-start | bytes 25165828 | tf_op jit(solution)/shard_map/while
  316.7 4.7 copy-start.4
  326.4 12.0 %copy-start.1 = (f32[2,8,256,128]{3,2,1,0:T(8,128)S(1)}, f32[2,8,256,128]{3,2,1,0:T(8,128)}, u32[]{:S(2)}) copy-start(f32[2,8,256,128]{3,2,1,0:T(8,128)} %get-tuple-element.444) | copy-start | bytes 6291460 | tf_op jit(solution)/shard_map/while
  332.6 5.9 %copy-start = (f32[2,512,256,8]{2,1,3,0:T(8,128)S(1)}, f32[2,512,256,8]{2,1,3,0:T(8,128)}, u32[]{:S(2)}) copy-start(f32[2,512,256,8]{2,1,3,0:T(8,128)} %get-tuple-element.424) | copy-start | bytes 25165828 | tf_op jit(solution)/shard_map/while
  337.2 4.7 copy-start.4
  346.9 12.0 %copy-start.1 = (f32[2,8,256,128]{3,2,1,0:T(8,128)S(1)}, f32[2,8,256,128]{3,2,1,0:T(8,128)}, u32[]{:S(2)}) copy-start(f32[2,8,256,128]{3,2,1,0:T(8,128)} %get-tuple-element.444) | copy-start | bytes 6291460 | tf_op jit(solution)/shard_map/while
  353.1 4.6 copy-start.3
  353.1 5.9 %copy-start = (f32[2,512,256,8]{2,1,3,0:T(8,128)S(1)}, f32[2,512,256,8]{2,1,3,0:T(8,128)}, u32[]{:S(2)}) copy-start(f32[2,512,256,8]{2,1,3,0:T(8,128)} %get-tuple-element.424) | copy-start | bytes 25165828 | tf_op jit(solution)/shard_map/while
  357.7 4.7 copy-start.4
  367.4 12.0 %copy-start.1 = (f32[2,8,256,128]{3,2,1,0:T(8,128)S(1)}, f32[2,8,256,128]{3,2,1,0:T(8,128)}, u32[]{:S(2)}) copy-start(f32[2,8,256,128]{3,2,1,0:T(8,128)} %get-tuple-element.444) | copy-start | bytes 6291460 | tf_op jit(solution)/shard_map/while
  373.6 5.9 %copy-start = (f32[2,512,256,8]{2,1,3,0:T(8,128)S(1)}, f32[2,512,256,8]{2,1,3,0:T(8,128)}, u32[]{:S(2)}) copy-start(f32[2,512,256,8]{2,1,3,0:T(8,128)} %get-tuple-element.424) | copy-start | bytes 25165828 | tf_op jit(solution)/shard_map/while
  378.2 4.7 copy-start.4
  387.9 12.0 %copy-start.1 = (f32[2,8,256,128]{3,2,1,0:T(8,128)S(1)}, f32[2,8,256,128]{3,2,1,0:T(8,128)}, u32[]{:S(2)}) copy-start(f32[2,8,256,128]{3,2,1,0:T(8,128)} %get-tuple-element.444) | copy-start | bytes 6291460 | tf_op jit(solution)/shard_map/while
  394.1 5.9 %copy-start = (f32[2,512,256,8]{2,1,3,0:T(8,128)S(1)}, f32[2,512,256,8]{2,1,3,0:T(8,128)}, u32[]{:S(2)}) copy-start(f32[2,512,256,8]{2,1,3,0:T(8,128)} %get-tuple-element.424) | copy-start | bytes 25165828 | tf_op jit(solution)/shard_map/while
  398.7 4.7 copy-start.4
  408.4 12.0 %copy-start.1 = (f32[2,8,256,128]{3,2,1,0:T(8,128)S(1)}, f32[2,8,256,128]{3,2,1,0:T(8,128)}, u32[]{:S(2)}) copy-start(f32[2,8,256,128]{3,2,1,0:T(8,128)} %get-tuple-element.444) | copy-start | bytes 6291460 | tf_op jit(solution)/shard_map/while
  414.6 5.9 %copy-start = (f32[2,512,256,8]{2,1,3,0:T(8,128)S(1)}, f32[2,512,256,8]{2,1,3,0:T(8,128)}, u32[]{:S(2)}) copy-start(f32[2,512,256,8]{2,1,3,0:T(8,128)} %get-tuple-element.424) | copy-start | bytes 25165828 | tf_op jit(solution)/shard_map/while
  419.2 4.7 copy-start.4
  428.9 12.0 %copy-start.1 = (f32[2,8,256,128]{3,2,1,0:T(8,128)S(1)}, f32[2,8,256,128]{3,2,1,0:T(8,128)}, u32[]{:S(2)}) copy-start(f32[2,8,256,128]{3,2,1,0:T(8,128)} %get-tuple-element.444) | copy-start | bytes 6291460 | tf_op jit(solution)/shard_map/while
  435.0 5.9 %copy-start = (f32[2,512,256,8]{2,1,3,0:T(8,128)S(1)}, f32[2,512,256,8]{2,1,3,0:T(8,128)}, u32[]{:S(2)}) copy-start(f32[2,512,256,8]{2,1,3,0:T(8,128)} %get-tuple-element.424) | copy-start | bytes 25165828 | tf_op jit(solution)/shard_map/while
  439.7 4.7 copy-start.4
  447.7 23.4 %copy-start.8 = (s32[32]{0:T(128)S(1)}, s32[32]{0:T(128)}, u32[]{:S(2)}) copy-start(s32[32]{0:T(128)} %copy-done.7) | copy-start | bytes 388
  448.9 32.5 %copy-start.5 = (f32[2,8,256]{2,1,0:T(8,128)S(1)}, f32[2,8,256]{2,1,0:T(8,128)}, u32[]{:S(2)}) copy-start(f32[2,8,256]{2,1,0:T(8,128)} %get-tuple-element.238) | copy-start | bytes 49156
  475.7 21.1 %all-to-all-start.3 = ((bf16[4,64,2048]{2,1,0:T(8,128)(2,1)}), bf16[4,64,2048]{2,1,0:T(8,128)(2,1)S(1)}, u32[]{:S(2)}, u32[]{:S(2)}) async-start(bf16[4,64,2048]{2,1,0:T(8,128)(2,1)} %bitcast.8), calls=%async_computation.3 | async-start | bytes 2097152 | tf_op jit(solution)/shard_map/all_to_all | solution.py:155
  (25 other events, 58.6 us)
Sparse Core Ops, SparseCore 0:
  10.2 84.6 all-gather.1
